TPU v7x, 32 devices: a whole 2x2x4 slice. The times are simulated.
32 devices in a mesh: groups: 2 (over x), dp: 4 (over y, core), region: 4 (over z).
Axes of the slice: x: 2, y: 2, z: 4, core: 2. Of those that a mesh axis runs over, the one named last changes fastest.
Arguments:
- features: bfloat16 [8, 16384, 256], P(('groups', 'dp'), 'region'), parts along dimension 0, may hold values from -6 to 6
- adjacency: bfloat16 [8, 384, 128, 128], P(('groups', 'dp'), 'region'), parts along dimension 0, may hold values from -0.3125 to 0.3125
- src_tiles: int32 [8, 384], P(('groups', 'dp'), 'region'), parts along dimension 0, may hold values from 0 to 39, as said below
- dst_tiles: int32 [8, 384], P(('groups', 'dp'), 'region'), parts along dimension 0, may hold values from 0 to 31
- counts: int32 [8, 4], P(('groups', 'dp'), 'region'), parts along dimension 0, may hold values from 1 to 96, as said below
- send_low: int32 [8, 16], P(('groups', 'dp'), 'region'), parts along dimension 0, may hold values from 0 to 31, as said below
- send_high: int32 [8, 16], P(('groups', 'dp'), 'region'), parts along dimension 0, may hold values from 0 to 31, as said below
- w_message: bfloat16 [256, 256], replicated, may hold values from -0.375 to 0.375
- w_update: bfloat16 [256, 256], replicated, may hold values from -0.375 to 0.375
- grad_out: bfloat16 [8, 16384, 256], P(('groups', 'dp'), 'region'), parts along dimension 0, may hold values from -6 to 6
Outputs:
- output: bfloat16 [8, 16384, 256], P(('groups', 'dp'), 'region'), parts along dimension 0
- grad_features: bfloat16 [8, 16384, 256], P(('groups', 'dp'), 'region'), parts along dimension 0
- grad_message: float32 [512, 256], P('groups'), parts along dimension 0
- grad_update: float32 [512, 256], P('groups'), parts along dimension 0
There are 2 independent parts, one for each index of `groups`. A program takes and returns all parts, laid end to end along the dimension named above; an argument that names none is the same for every part. Nothing has to cross between parts.
Inputs may be any that keep to these rules, and one draw needn't show every extreme that they name: `src_tiles`: index into a region's extended list of 40 tiles. `counts`: in each event one region has all 96 slots live. `send_low`: the 4 entries of one region are distinct. `send_high`: the 4 entries of one region are distinct.
All inputs are finite; a program needn't handle non-finite values.
Results may differ from a plain program's by a relative error of at most 0.007.
Values may be sent and summed in bfloat16 or wider, within the bound.
A program may use at most 128 MiB of HBM per device.

v0:
```python
import math

import jax
import jax.numpy as jnp
from jax import lax
from jax.sharding import PartitionSpec as P


def with_halo(cells, sides, width):
    for axis, dim in sides:
        count = lax.axis_size(axis)
        head = lax.slice_in_dim(cells, 0, width, axis=dim)
        tail = lax.slice_in_dim(cells, cells.shape[dim] - width, cells.shape[dim], axis=dim)
        cells = jnp.concatenate(
            [
                lax.ppermute(tail, axis, [(i, (i + 1) % count) for i in range(count)]),
                cells,
                lax.ppermute(head, axis, [((i + 1) % count, i) for i in range(count)]),
            ],
            axis=dim,
        )
    return cells


def body(
    features,
    adjacency,
    src_tiles,
    dst_tiles,
    counts,
    send_low,
    send_high,
    w_message,
    w_update,
    grad_out,
):
    tile = adjacency.shape[-1]
    slots = adjacency.shape[1]
    width = features.shape[-1]
    x_rows = features[0]
    ntile = x_rows.shape[0] // tile
    bound = send_low.shape[1]
    lows = send_low[0]
    highs = send_high[0]
    message = jnp.dot(x_rows, w_message, preferred_element_type=jnp.float32).astype(jnp.bfloat16)
    msg_tiles = message.reshape(ntile, tile, width)
    rims = jnp.concatenate([msg_tiles[lows], msg_tiles[highs]], axis=0)
    padded = with_halo(rims, (("region", 0),), bound)
    halo_tiles = jnp.concatenate([padded[:bound], padded[-bound:]], axis=0)
    extended = jnp.concatenate([msg_tiles, halo_tiles], axis=0)
    live = (jnp.arange(slots) < counts[0, 0]).astype(jnp.float32)
    src = src_tiles[0]
    dst = dst_tiles[0]
    adj = adjacency[0]
    gathered = extended[src]
    contrib = jnp.einsum("kij,kjd->kid", adj, gathered, preferred_element_type=jnp.float32)
    aggregate = (
        jnp.zeros((ntile, tile, width), jnp.float32).at[dst].add(contrib * live[:, None, None])
    )
    aggregate = aggregate.astype(jnp.bfloat16).reshape(-1, width)
    update = jnp.dot(aggregate, w_update, preferred_element_type=jnp.float32)
    sig = jax.nn.sigmoid(update)
    output = (x_rows.astype(jnp.float32) + update * sig).astype(jnp.bfloat16)
    g_rows = grad_out[0]
    grad_in = (g_rows.astype(jnp.float32) * sig * (1.0 + update * (1.0 - sig))).astype(jnp.bfloat16)
    part_update = lax.dot_general(
        aggregate, grad_in, (((0,), (0,)), ((), ())), preferred_element_type=jnp.float32
    )
    grad_agg = lax.dot_general(
        grad_in, w_update, (((1,), (1,)), ((), ())), preferred_element_type=jnp.float32
    )
    grad_agg = grad_agg.astype(jnp.bfloat16).reshape(ntile, tile, width)
    picked = grad_agg[dst]
    back = jnp.einsum("kij,kid->kjd", adj, picked, preferred_element_type=jnp.float32)
    grad_ext = (
        jnp.zeros((ntile + 2 * bound, tile, width), jnp.float32)
        .at[src]
        .add(back * live[:, None, None])
    )
    rims_back = grad_ext[ntile:]
    padded_back = with_halo(rims_back, (("region", 0),), bound)
    from_lower = padded_back[:bound]
    from_upper = padded_back[-bound:]
    grad_msg = grad_ext[:ntile]
    grad_msg = grad_msg.at[lows].add(from_lower)
    grad_msg = grad_msg.at[highs].add(from_upper)
    grad_msg = grad_msg.astype(jnp.bfloat16).reshape(-1, width)
    part_message = lax.dot_general(
        x_rows, grad_msg, (((0,), (0,)), ((), ())), preferred_element_type=jnp.float32
    )
    grad_features = (
        g_rows.astype(jnp.float32)
        + lax.dot_general(
            grad_msg, w_message, (((1,), (1,)), ((), ())), preferred_element_type=jnp.float32
        )
    ).astype(jnp.bfloat16)
    sum_message, sum_update = lax.psum((part_message, part_update), ("dp", "region"))
    scale = 1.0 / math.sqrt(lax.axis_size("dp") * lax.axis_size("region") * x_rows.shape[0])
    return (output[None], grad_features[None], sum_message * scale, sum_update * scale)


def solution(mesh):
    in_specs = (
        P(("groups", "dp"), "region", None),
        P(("groups", "dp"), "region", None, None),
        P(("groups", "dp"), "region"),
        P(("groups", "dp"), "region"),
        P(("groups", "dp"), "region"),
        P(("groups", "dp"), "region"),
        P(("groups", "dp"), "region"),
        P(),
        P(),
        P(("groups", "dp"), "region", None),
    )
    out_specs = (
        P(("groups", "dp"), "region", None),
        P(("groups", "dp"), "region", None),
        P("groups", None),
        P("groups", None),
    )
    return jax.shard_map(body, mesh=mesh, in_specs=in_specs, out_specs=out_specs, check_vma=False)
```

profile of v0, /device:TPU:0, one launch (start us, length us, event | category | flops | bytes accessed | tf_op | source)
XLA Modules:
  0.0 306.7 jit_solution(6473691448623572954)
XLA Ops:
  7.2 0.0 copy-start
  7.2 0.0 copy-start.11
  7.2 0.0 all-reduce.3.cloned.1.call-start
  7.3 0.8 fusion.14
  8.1 3.7 %convolution_convert_fusion.1 = bf16[4096,256]{1,0:T(8,128)(2,1)} fusion(bf16[256,256]{1,0:T(8,128)(2,1)} %param.17, bf16[1,4096,256]{2,1,0:T(8,128)(2,1)} %param.10), kind=kOutput, calls=%fused_computation.14 | convolution fusion | flops 537919488 | bytes 4325376 | tf_op jit(solution)/shard_map/dot_general | solution.py:45
  11.8 2.9 gather_fusion
  14.7 3.0 collective-permute-start
  17.7 2.9 gather_fusion.1
  20.5 2.0 collective-permute-start.1
  23.3 3.7 %collective-permute-done = bf16[4,128,256]{2,1,0:T(8,128)(2,1)S(1)} collective-permute-done((bf16[4,128,256]{2,1,0:T(8,128)(2,1)}, bf16[4,128,256]{2,1,0:T(8,128)(2,1)S(1)}, u32[]{:S(2)}, u32[]{:S(2)}) %collective-permute-start) | collective-permute-done | bytes 262176 | tf_op jit(solution)/shard_map/ppermute | solution.py:16
  27.1 4.8 %collective-permute-done.1 = bf16[4,128,256]{2,1,0:T(8,128)(2,1)S(1)} collective-permute-done((bf16[4,128,256]{2,1,0:T(8,128)(2,1)}, bf16[4,128,256]{2,1,0:T(8,128)(2,1)S(1)}, u32[]{:S(2)}, u32[]{:S(2)}) %collective-permute-start.1) | collective-permute-done | bytes 262176 | tf_op jit(solution)/shard_map/ppermute | solution.py:18
  31.8 3.5 %pad_maximum_fusion = bf16[40,128,256]{2,1,0:T(8,128)(2,1)} fusion(bf16[4,128,256]{2,1,0:T(8,128)(2,1)S(1)} %collective-permute-done.1, bf16[4,128,256]{2,1,0:T(8,128)(2,1)S(1)} %collective-permute-done, bf16[32,128,256]{2,1,0:T(8,128)(2,1)} %bitcast.66), kind=kLoop, calls=%fused_computation.22 | loop fusion | flops 2621440 | bytes 5242880 | tf_op jit(solution)/shard_map/concatenate | solution.py:50
  35.3 7.7 %gather_fusion.2 = bf16[96,128,256]{2,1,0:T(8,128)(2,1)} fusion(bf16[40,128,256]{2,1,0:T(8,128)(2,1)} %pad_maximum_fusion, s32[1024]{0:T(1024)S(1)} %pad_clamp_fusion.1), kind=kCustom, calls=%fused_computation.2 | custom fusion | bytes 12583296 | tf_op jit(solution)/shard_map/gather | solution.py:55
  43.0 9.8 %multiply_bitcast_fusion.1 = f32[96,128,256]{1,2,0:T(8,128)} fusion(f32[96]{0:T(128)S(1)} %compare_convert_fusion, bf16[96,128,256]{2,1,0:T(8,128)(2,1)} %gather_fusion.2, bf16[1,96,128,128]{3,2,1,0:T(8,128)(2,1)S(1)} %copy-done), kind=kOutput, calls=%fused_computation.9 | convolution fusion | flops 808452096 | bytes 22020480 | tf_op jit(solution)/shard_map/kij,kjd->kid/dot_general | solution.py:56
  52.9 12.6 %copy.20 = f32[96,128,256]{2,1,0:T(8,128)} copy(f32[96,128,256]{1,2,0:T(8,128)} %multiply_bitcast_fusion.1) | data formatting | bytes 25165824 | tf_op jit(solution)/shard_map/mul | solution.py:58
  65.5 2.4 broadcast_in_dim.8
  67.9 28.6 %scatter_fusion = f32[32,128,256]{2,1,0:T(8,128)} fusion(f32[32,128,256]{2,1,0:T(8,128)} %broadcast_in_dim.8, s32[96]{0:T(128)S(1)} %fusion.13, f32[96,128,256]{2,1,0:T(8,128)} %copy.20), kind=kCustom, calls=%fused_computation.4 | custom fusion | flops 3145728 | bytes 37749120 | tf_op jit(solution)/shard_map/scatter-add | solution.py:58
  96.5 2.6 convert_element_type.41
  99.1 0.2 copy-done.3
  99.3 0.6 copy-done.6
  99.9 3.6 %fusion.3 = (bf16[4096,256]{1,0:T(8,128)(2,1)S(1)}, bf16[1,4096,256]{2,1,0:T(8,128)(2,1)}) fusion(bf16[1,4096,256]{2,1,0:T(8,128)(2,1)S(1)} %copy-done.6, bf16[1,4096,256]{2,1,0:T(8,128)(2,1)S(1)} %copy-done.3, bf16[4096,256]{1,0:T(8,128)(2,1)S(1)} %bitcast.69, bf16[256,256]{1,0:T(8,128)(2,1)S(1)} %copy-done.10), kind=kOutput, calls=%fused_computation.17 | convolution fusion | flops 551550976 | bytes 10616832 | tf_op jit(solution)/shard_map/dot_general | solution.py:61
  103.6 1.3 copy-done.4
  104.9 2.1 convolution_convert_fusion
  107.0 7.6 %gather_fusion.3 = bf16[96,128,256]{2,1,0:T(8,128)(2,1)} fusion(bf16[32,128,256]{2,1,0:T(8,128)(2,1)} %bitcast.63, s32[1024]{0:T(1024)S(1)} %pad_clamp_fusion), kind=kCustom, calls=%fused_computation.3 | custom fusion | bytes 12583296 | tf_op jit(solution)/shard_map/gather | solution.py:73
  114.6 9.8 %multiply_bitcast_fusion = f32[96,128,256]{1,2,0:T(8,128)} fusion(f32[96]{0:T(128)S(1)} %compare_convert_fusion, bf16[96,128,256]{2,1,0:T(8,128)(2,1)} %gather_fusion.3, bf16[1,96,128,128]{3,2,1,0:T(8,128)(2,1)S(1)} %copy-done), kind=kOutput, calls=%fused_computation.8 | convolution fusion | flops 808452096 | bytes 22020480 | tf_op jit(solution)/shard_map/kij,kid->kjd/dot_general | solution.py:74
  124.4 12.6 %copy.22 = f32[96,128,256]{2,1,0:T(8,128)} copy(f32[96,128,256]{1,2,0:T(8,128)} %multiply_bitcast_fusion) | data formatting | bytes 25165824 | tf_op jit(solution)/shard_map/mul | solution.py:78
  137.0 2.9 broadcast_in_dim.10
  139.9 28.8 %scatter_fusion.1 = f32[40,128,256]{2,1,0:T(8,128)} fusion(f32[40,128,256]{2,1,0:T(8,128)} %broadcast_in_dim.10, s32[96]{0:T(128)S(1)} %fusion.16, f32[96,128,256]{2,1,0:T(8,128)} %copy.22), kind=kCustom, calls=%fused_computation.5 | custom fusion | flops 3145728 | bytes 37749120 | tf_op jit(solution)/shard_map/scatter-add | solution.py:78
  168.7 2.1 fusion.17
  170.8 0.4 collective-permute-start.2
  171.2 3.5 %collective-permute-start.3 = (f32[4,128,256]{2,1,0:T(8,128)}, f32[4,128,256]{2,1,0:T(8,128)S(1)}, u32[]{:S(2)}, u32[]{:S(2)}) collective-permute-start(f32[4,128,256]{2,1,0:T(8,128)} %get-tuple-element.14), channel_id=1, source_target_pairs={{1,0},{2,1},{3,2},{0,3},{5,4},{6,5},{7,6},{4,7},{9,8},{10,9},{11,1... | collective-permute-start | bytes 1572872 | tf_op jit(solution)/shard_map/ppermute | solution.py:18
  174.6 4.6 %slice.23 = f32[32,128,256]{2,1,0:T(8,128)} slice(f32[40,128,256]{2,1,0:T(8,128)} %scatter_fusion.1), slice={[0:32], [0:128], [0:256]} | slice | bytes 8388608 | tf_op jit(solution)/shard_map/slice | solution.py:84
  179.2 1.6 fusion.18
  180.9 6.6 %collective-permute-done.2 = f32[4,128,256]{2,1,0:T(8,128)S(1)} collective-permute-done((f32[4,128,256]{2,1,0:T(8,128)S(1)}, f32[4,128,256]{2,1,0:T(8,128)S(1)}, u32[]{:S(2)}, u32[]{:S(2)}) %collective-permute-start.2) | collective-permute-done | bytes 524320 | tf_op jit(solution)/shard_map/ppermute | solution.py:16
  187.4 2.7 scatter_fusion.2
  190.1 5.8 %collective-permute-done.3 = f32[4,128,256]{2,1,0:T(8,128)S(1)} collective-permute-done((f32[4,128,256]{2,1,0:T(8,128)}, f32[4,128,256]{2,1,0:T(8,128)S(1)}, u32[]{:S(2)}, u32[]{:S(2)}) %collective-permute-start.3) | collective-permute-done | bytes 524320 | tf_op jit(solution)/shard_map/ppermute | solution.py:18
  195.9 2.7 scatter_fusion.3
  198.6 2.5 convert_element_type.47
  201.1 0.0 copy-start.9
  201.1 1.3 copy-done.2
  202.4 3.0 fusion.10
  205.5 0.0 all-reduce.3.cloned.1.call-update
  205.5 0.0 copy-start.1
  205.5 4.4 %fusion.1 = bf16[1,4096,256]{2,1,0:T(8,128)(2,1)} fusion(bf16[4096,256]{1,0:T(8,128)(2,1)} %bitcast.68, bf16[256,256]{1,0:T(8,128)(2,1)S(1)} %copy-done.9, bf16[1,4096,256]{2,1,0:T(8,128)(2,1)} %param.19), kind=kOutput, calls=%fused_computation.15 | convolution fusion | flops 540016640 | bytes 6422528 | tf_op jit(solution)/shard_map/dot_general | solution.py:93
  210.0 85.5 %all-reduce.3.cloned.1.call-done = (f32[256,256]{0,1:T(8,128)}, f32[256,256]{0,1:T(8,128)}) async-done(((f32[256,256]{0,1:T(8,128)}, f32[256,256]{0,1:T(8,128)}), (f32[256,256]{0,1:T(8,128)}, f32[256,256]{0,1:T(8,128)})) %all-reduce.3.cloned.1.call-update) | async-done | bytes 524304 | tf_op jit(solution)/shard_map/psum | solution.py:97
  295.5 1.8 broadcast_multiply_fusion
  297.2 1.8 copy.24
  299.0 0.8 copy.25
  (28 shorter events, 0.1 us)
Async XLA Ops:
  7.2 35.9 %copy-start = (bf16[1,96,128,128]{3,2,1,0:T(8,128)(2,1)S(1)}, bf16[1,96,128,128]{3,2,1,0:T(8,128)(2,1)}, u32[]{:S(2)}) copy-start(bf16[1,96,128,128]{3,2,1,0:T(8,128)(2,1)} %param.11) | copy-start | bytes 9437188
  7.2 10.5 %copy-start.11 = (s32[1,4]{1,0:T(1,128)S(1)}, s32[1,4]{1,0:T(1,128)}, u32[]{:S(2)}) copy-start(s32[1,4]{1,0:T(1,128)} %param.15) | copy-start | bytes 52
  7.2 15.4 %copy-start.12 = (s32[1,96]{1,0:T(1,128)S(1)}, s32[1,96]{1,0:T(1,128)}, u32[]{:S(2)}) copy-start(s32[1,96]{1,0:T(1,128)} %param.12) | copy-start | bytes 1156
  7.2 16.1 %copy-start.13 = (s32[1,96]{1,0:T(1,128)S(1)}, s32[1,96]{1,0:T(1,128)}, u32[]{:S(2)}) copy-start(s32[1,96]{1,0:T(1,128)} %param.13) | copy-start | bytes 1156
  7.2 288.2 %all-reduce.3.cloned.1.call-start = ((), (), s32[]{:S(2)}) async-start(), calls=%async_computation | async-start | bytes 1048576 | tf_op jit(solution)/shard_map/psum | solution.py:97
  14.7 12.4 %collective-permute-start = (bf16[4,128,256]{2,1,0:T(8,128)(2,1)}, bf16[4,128,256]{2,1,0:T(8,128)(2,1)S(1)}, u32[]{:S(2)}, u32[]{:S(2)}) collective-permute-start(bf16[4,128,256]{2,1,0:T(8,128)(2,1)} %gather_fusion), channel_id=1, source_target_pairs={{0,1},{1,2},{2,3},{3,0},{4,5},{5,6},{6,7},{7,4},{8,9},{9,10},{10,1... | collective-permute-start | bytes 786440 | tf_op jit(solution)/shard_map/ppermute | solution.py:16
  20.5 11.3 %collective-permute-start.1 = (bf16[4,128,256]{2,1,0:T(8,128)(2,1)}, bf16[4,128,256]{2,1,0:T(8,128)(2,1)S(1)}, u32[]{:S(2)}, u32[]{:S(2)}) collective-permute-start(bf16[4,128,256]{2,1,0:T(8,128)(2,1)} %gather_fusion.1), channel_id=1, source_target_pairs={{1,0},{2,1},{3,2},{0,3},{5,4},{6,5},{7,6},{4,7},{9,8},{10,9},{11,1... | collective-permute-start | bytes 786440 | tf_op jit(solution)/shard_map/ppermute | solution.py:18
  96.5 2.9 copy-start.3
  96.5 3.5 %copy-start.6 = (bf16[1,4096,256]{2,1,0:T(8,128)(2,1)S(1)}, bf16[1,4096,256]{2,1,0:T(8,128)(2,1)}, u32[]{:S(2)}) copy-start(bf16[1,4096,256]{2,1,0:T(8,128)(2,1)} %param.19) | copy-start | bytes 6291460
  96.5 3.5 %copy-start.10 = (bf16[256,256]{1,0:T(8,128)(2,1)S(1)}, bf16[256,256]{1,0:T(8,128)(2,1)}, u32[]{:S(2)}) copy-start(bf16[256,256]{1,0:T(8,128)(2,1)} %param.18) | copy-start | bytes 393220
  99.1 4.5 %copy-start.7 = (bf16[32,128,256]{2,1,0:T(8,128)(2,1)}, bf16[32,128,256]{2,1,0:T(8,128)(2,1)S(1)}, u32[]{:S(2)}) copy-start(bf16[32,128,256]{2,1,0:T(8,128)(2,1)S(1)} %convert_element_type.41) | copy-start | bytes 6291460
  103.6 1.3 copy-start.4
  170.8 16.6 %collective-permute-start.2 = (f32[4,128,256]{2,1,0:T(8,128)S(1)}, f32[4,128,256]{2,1,0:T(8,128)S(1)}, u32[]{:S(2)}, u32[]{:S(2)}) collective-permute-start(f32[4,128,256]{2,1,0:T(8,128)S(1)} %get-tuple-element.15), channel_id=1, source_target_pairs={{0,1},{1,2},{2,3},{3,0},{4,5},{5,6},{6,7},{7,4},{8,9},{9,10},{10,1... | collective-permute-start | bytes 1572872 | tf_op jit(solution)/shard_map/ppermute | solution.py:16
  171.2 8.1 %copy-start.5 = (bf16[4096,256]{1,0:T(8,128)(2,1)S(1)}, bf16[4096,256]{1,0:T(8,128)(2,1)}, u32[]{:S(2)}) copy-start(bf16[4096,256]{1,0:T(8,128)(2,1)} %copy-done.4) | copy-start | bytes 6291460
  171.2 8.1 %copy-start.8 = (bf16[32,128,256]{2,1,0:T(8,128)(2,1)S(1)}, bf16[32,128,256]{2,1,0:T(8,128)(2,1)}, u32[]{:S(2)}) copy-start(bf16[32,128,256]{2,1,0:T(8,128)(2,1)} %copy-done.7) | copy-start | bytes 6291460
  171.2 24.8 %collective-permute-start.3 = (f32[4,128,256]{2,1,0:T(8,128)}, f32[4,128,256]{2,1,0:T(8,128)S(1)}, u32[]{:S(2)}, u32[]{:S(2)}) collective-permute-start(f32[4,128,256]{2,1,0:T(8,128)} %get-tuple-element.14), channel_id=1, source_target_pairs={{1,0},{2,1},{3,2},{0,3},{5,4},{6,5},{7,6},{4,7},{9,8},{10,9},{11,1... | collective-permute-start | bytes 1572872 | tf_op jit(solution)/shard_map/ppermute | solution.py:18
  201.1 1.3 copy-start.2
  201.1 4.4 %copy-start.9 = (bf16[256,256]{1,0:T(8,128)(2,1)S(1)}, bf16[256,256]{1,0:T(8,128)(2,1)}, u32[]{:S(2)}) copy-start(bf16[256,256]{1,0:T(8,128)(2,1)} %param.17) | copy-start | bytes 393220
  205.5 94.3 %copy-start.1 = (bf16[1,96,128,128]{3,2,1,0:T(8,128)(2,1)S(1)}, bf16[1,96,128,128]{3,2,1,0:T(8,128)(2,1)}, u32[]{:S(2)}) copy-start(bf16[1,96,128,128]{3,2,1,0:T(8,128)(2,1)} %param.11) | copy-start | bytes 9437188
Sparse Core Ops, SparseCore 0:
  205.6 89.7 all-reduce.2
where the time goes:
time: 308 us; the launch traced here: 307 us
  waiting for transfers between devices  106 us (34%)
  other arithmetic  73.9 us (24%)
  local copies, waits for them, and re-layouts  64.3 us (21%)
  matrix products  38.2 us (12%)
  between operations  14.8 us (5%)
  starting transfers between devices  8.93 us (3%)
    psum x1, waiting for transfers between devices, body(): lax.psum((part_message, part_update), ('dp', 'region'))  85.5 us
    scatter-add x1, other arithmetic, body(): grad_ext = jnp.zeros((ntile + 2 * bound, tile, width), jnp.float32).at[sr...  28.8 us
    scatter-add x1, other arithmetic, body(): jnp.zeros((ntile, tile, width), jnp.float32).at[dst]  28.6 us
    mul x1, local copies, waits for them, and re-layouts, body(): contrib * live[:, None, None]  12.6 us
    mul x1, local copies, waits for them, and re-layouts, body(): back * live[:, None, None]  12.6 us
    ppermute x2, waiting for transfers between devices, with_halo(): lax.ppermute(head, axis, [((i + 1) % count, i) for i in range(count)])  10.6 us
    ppermute x2, waiting for transfers between devices, with_halo(): lax.ppermute(tail, axis, [(i, (i + 1) % count) for i in range(count)])  10.3 us
    dot_general x1, matrix products, body(): jnp.einsum('kij,kid->kjd', adj, picked, preferred_element_type=jnp.float32)  9.85 us
  transfers between devices with their start and end apart: 5, of which 5 were waited for; matrix products, arithmetic and copies ran while one was open for 5% of the time, Pallas kernels for 0%

commit v1 on v0

v1 whole, which is shorter than its diff:
```python
import functools
import math

import jax
import jax.numpy as jnp
from jax import lax
from jax.experimental import pallas as pl
from jax.experimental.pallas import tpu as pltpu
from jax.sharding import PartitionSpec as P

MESH = pl.DeviceIdType.MESH
F32 = jnp.float32
BF16 = jnp.bfloat16
WIRE = jnp.bfloat16
GROUP = 8


def dot(a, b, ca=1, cb=0):
    return lax.dot_general(a, b, (((ca,), (cb,)), ((), ())), preferred_element_type=F32)


def order_rows(key, other, lanes, subs):
    full = key.shape[1]
    key_l = jnp.broadcast_to(key, (full, full))
    key_s = key_l.T
    other_s = jnp.broadcast_to(other, (full, full)).T
    before = (key_s < key_l) | ((key_s == key_l) & (subs < lanes))
    rank = jnp.sum(before.astype(jnp.int32), axis=0, keepdims=True)
    hit = jnp.broadcast_to(rank, (full, full)).T == lanes
    perm = jnp.sum(jnp.where(hit, subs, 0), axis=0, keepdims=True)
    moved = jnp.sum(jnp.where(hit, other_s, 0), axis=0, keepdims=True)
    keys = jnp.sum(jnp.where(hit, key_s, 0), axis=0, keepdims=True)
    keep = (keys == pltpu.roll(keys, 1, axis=1)).astype(jnp.int32)
    upto = jnp.sum((key_s <= lanes).astype(jnp.int32), axis=0, keepdims=True)
    under = jnp.sum((key_s < lanes).astype(jnp.int32), axis=0, keepdims=True)
    last = jnp.where(upto > under, upto, 0)
    return perm, moved, keep, last


def kernel(
    n_dp,
    n_rg,
    scale,
    counts,
    lows,
    highs,
    src_ref,
    dst_ref,
    x_hbm,
    adj_hbm,
    g_hbm,
    wm,
    wu,
    out_hbm,
    gf_hbm,
    sm_ref,
    su_ref,
    x,
    adj,
    g,
    ext,
    halo,
    sent,
    runs,
    gagg,
    out_v,
    gf_v,
    rim_s,
    rim_r,
    pad,
    tab_v,
    tab,
    total,
    wire1,
    recv1,
    wire2,
    wire3,
    load_sem,
    tab_sem,
    store_sem,
    hs_sem,
    hr_sem,
    bs_sem,
    br_sem,
    s1,
    r1,
    s2,
    r2,
    s3,
    r3,
):
    slots, tile = adj.shape[0], adj.shape[1]
    ntile, _, width = x.shape
    cells = ntile * tile
    bound = lows.shape[1]
    rows = width // n_dp
    dp = lax.axis_index("dp")
    rg = lax.axis_index("region")
    up, down = lax.rem(rg + 1, n_rg), lax.rem(rg + n_rg - 1, n_rg)

    loads = [
        pltpu.make_async_copy(a, b, load_sem.at[i])
        for i, (a, b) in enumerate(((x_hbm, x), (adj_hbm, adj), (g_hbm, g)))
    ]
    for c in loads:
        c.start()

    barrier = pltpu.get_barrier_semaphore()
    for off in range(1, n_dp):
        pl.semaphore_signal(barrier, inc=1, device_id={"dp": lax.rem(dp + off, n_dp)}, device_id_type=MESH)
    for off in range(1, n_rg):
        pl.semaphore_signal(barrier, inc=1, device_id={"region": lax.rem(rg + off, n_rg)}, device_id_type=MESH)
    pl.semaphore_wait(barrier, n_dp + n_rg - 2)

    loads[0].wait()
    for i in range(bound):
        sent[bound + i] = x[highs[0, i]]
    to_up = pltpu.make_async_remote_copy(
        sent.at[pl.ds(bound, bound)], halo.at[pl.ds(0, bound)], hs_sem.at[0], hr_sem.at[0],
        device_id={"region": up}, device_id_type=MESH)
    to_up.start()
    for i in range(bound):
        sent[i] = x[lows[0, i]]
    to_down = pltpu.make_async_remote_copy(
        sent.at[pl.ds(0, bound)], halo.at[pl.ds(bound, bound)], hs_sem.at[1], hr_sem.at[1],
        device_id={"region": down}, device_id_type=MESH)
    to_down.start()

    full = pad.shape[1]
    pad[...] = jnp.zeros_like(pad)
    pad[0:1, 0:slots] = src_ref[...]
    pad[1:2, 0:slots] = dst_ref[...]
    lanes = lax.broadcasted_iota(jnp.int32, (full, full), 1)
    subs = lax.broadcasted_iota(jnp.int32, (full, full), 0)
    lane = lax.broadcasted_iota(jnp.int32, (1, full), 1)
    live = lane < counts[0, 0]
    in_slots = lane < slots
    src, dst = pad[0:1, :], pad[1:2, :]
    next_ = ntile + 2 * bound
    key_d = jnp.where(in_slots, jnp.where(live, dst, ntile), ntile + 1)
    key_s = jnp.where(in_slots, jnp.where(live, src, next_), next_ + 1)
    made = order_rows(key_d, src, lanes, subs) + order_rows(key_s, dst, lanes, subs)
    hi = jnp.full((1, full), 2 * bound, jnp.int32)
    lo = jnp.full((1, full), 2 * bound, jnp.int32)
    for i in range(bound):
        hi = jnp.where(lane == highs[0, i], bound + i, hi)
        lo = jnp.where(lane == lows[0, i], i, lo)
    tab_v[...] = jnp.zeros_like(tab_v)
    for i, row in enumerate(made + (hi, lo)):
        tab_v[i : i + 1, :] = row
    to_smem = pltpu.make_async_copy(tab_v, tab, tab_sem)
    to_smem.start()

    def rows_of(v):
        return v.reshape(-1, width)

    def tiles_of(v):
        return v.reshape(-1, tile, width)

    def message(c, _):
        at = pl.ds(4 * c, 4)
        ext[at] = tiles_of(dot(rows_of(x[at]), wm[...]).astype(BF16))
        return 0

    lax.fori_loop(0, ntile // 4, message, 0)
    runs[0] = jnp.zeros(runs.shape[1:], F32)
    rim_r[2 * bound] = jnp.zeros((tile, width), BF16)
    to_smem.wait()
    loads[1].wait()
    loads[2].wait()
    to_up.wait()
    to_down.wait()
    ext[pl.ds(ntile, 2 * bound)] = tiles_of(dot(rows_of(halo[...]), wm[...]).astype(BF16))

    def forward(b, _):
        acc = runs[b * GROUP]
        for u in range(GROUP):
            j = b * GROUP + u
            part = dot(adj[tab[0, j]], ext[tab[1, j]])
            acc = acc * tab[2, j].astype(F32) + part
            runs[j + 1] = acc
        return 0

    lax.fori_loop(0, slots // GROUP, forward, 0)

    total[0] = jnp.zeros((width, width), F32)

    def middle(c, _):
        at = pl.ds(2 * c, 2)
        agg = jnp.concatenate([runs[tab[3, 2 * c]], runs[tab[3, 2 * c + 1]]], axis=0).astype(BF16)
        update = dot(agg, wu[...])
        sig = jax.nn.sigmoid(update)
        out_v[at] = tiles_of((rows_of(x[at]).astype(F32) + update * sig).astype(BF16))
        gin = (rows_of(g[at]).astype(F32) * sig * (1.0 + update * (1.0 - sig))).astype(BF16)
        total[0] += dot(agg, gin, 0, 0)
        gagg[at] = tiles_of(dot(gin, wu[...], 1, 1).astype(BF16))
        return 0

    lax.fori_loop(0, ntile // 2, middle, 0)
    store_out = pltpu.make_async_copy(out_v, out_hbm, store_sem.at[0])
    store_out.start()

    def my_rows(d):
        return pl.ds(pl.multiple_of(d * rows, rows), rows)

    def spread(m):
        wire1[m] = total[m].astype(WIRE)
        copies = []
        for off in range(1, n_dp):
            to = lax.rem(dp + off, n_dp)
            copies.append(pltpu.make_async_remote_copy(
                wire1.at[m, my_rows(to)], recv1.at[m, off - 1], s1.at[m, off - 1], r1.at[m, off - 1],
                device_id={"dp": to}, device_id_type=MESH))
            copies[-1].start()
        return copies

    def across(m, copies):
        for c in copies:
            c.wait()
        part = total[m, my_rows(dp), :]
        for off in range(1, n_dp):
            part = part + recv1[m, off - 1].astype(F32)
        wire2[m, rg] = part.astype(WIRE)
        out = []
        for off in range(1, n_rg):
            out.append(pltpu.make_async_remote_copy(
                wire2.at[m, rg], wire2.at[m, rg], s2.at[m, off - 1], r2.at[m, off - 1],
                device_id={"region": lax.rem(rg + off, n_rg)}, device_id_type=MESH))
            out[-1].start()
        return out

    def back(m, copies):
        for c in copies:
            c.wait()
        part = wire2[m, 0].astype(F32)
        for q in range(1, n_rg):
            part = part + wire2[m, q].astype(F32)
        wire3[m, dp] = (part * scale).astype(WIRE)
        out = []
        for off in range(1, n_dp):
            out.append(pltpu.make_async_remote_copy(
                wire3.at[m, dp], wire3.at[m, dp], s3.at[m, off - 1], r3.at[m, off - 1],
                device_id={"dp": lax.rem(dp + off, n_dp)}, device_id_type=MESH))
            out[-1].start()
        return out

    def finish(m, copies, ref):
        for c in copies:
            c.wait()
        for d in range(n_dp):
            ref[d * rows : (d + 1) * rows, :] = wire3[m, d].astype(F32)

    u1 = spread(0)

    def backward(b, _):
        acc = runs[b * GROUP]
        for u in range(GROUP):
            j = b * GROUP + u
            part = dot(adj[tab[4, j]], gagg[tab[5, j]], 0, 0)
            acc = acc * tab[6, j].astype(F32) + part
            runs[j + 1] = acc
        return 0

    lax.fori_loop(0, slots // GROUP, backward, 0)
    for i in range(2 * bound):
        rim_s[i] = runs[tab[7, ntile + i]].astype(BF16)
    rim_down = pltpu.make_async_remote_copy(
        rim_s.at[pl.ds(0, bound)], rim_r.at[pl.ds(bound, bound)], bs_sem.at[0], br_sem.at[0],
        device_id={"region": down}, device_id_type=MESH)
    rim_up = pltpu.make_async_remote_copy(
        rim_s.at[pl.ds(bound, bound)], rim_r.at[pl.ds(0, bound)], bs_sem.at[1], br_sem.at[1],
        device_id={"region": up}, device_id_type=MESH)
    rim_down.start()
    rim_up.start()
    u2 = across(0, u1)

    total[1] = jnp.zeros((width, width), F32)

    def own(c, _):
        at = pl.ds(2 * c, 2)
        gm = jnp.concatenate([runs[tab[7, 2 * c]], runs[tab[7, 2 * c + 1]]], axis=0).astype(BF16)
        total[1] += dot(rows_of(x[at]), gm, 0, 0)
        return 0

    lax.fori_loop(0, ntile // 2, own, 0)
    u3 = back(0, u2)
    rim_down.wait()
    rim_up.wait()
    total[1] += dot(rows_of(sent[...]), rows_of(rim_r[pl.ds(0, 2 * bound)]), 0, 0)
    m1 = spread(1)

    def features(c):
        at = pl.ds(2 * c, 2)
        parts = []
        for u in range(2):
            t = 2 * c + u
            parts.append(
                runs[tab[7, t]]
                + rim_r[tab[8, t]].astype(F32)
                + rim_r[tab[9, t]].astype(F32)
            )
        gm = jnp.concatenate(parts, axis=0).astype(BF16)
        gf_v[at] = tiles_of((rows_of(g[at]).astype(F32) + dot(gm, wm[...], 1, 1)).astype(BF16))

    pairs = ntile // 2
    third = pairs // 3

    def some(lo_, hi_):
        def step(c, _):
            features(c)
            return 0

        lax.fori_loop(lo_, hi_, step, 0)

    some(0, third)
    m2 = across(1, m1)
    some(third, pairs)
    store_gf = pltpu.make_async_copy(gf_v, gf_hbm, store_sem.at[1])
    store_gf.start()
    finish(0, u3, su_ref)
    m3 = back(1, m2)
    finish(1, m3, sm_ref)
    store_out.wait()
    store_gf.wait()


def body(n_dp, n_rg, features, adjacency, src_tiles, dst_tiles, counts, send_low, send_high,
         w_message, w_update, grad_out):
    slots, tile = adjacency.shape[1], adjacency.shape[-1]
    cells, width = features.shape[1:]
    bound = send_low.shape[1]
    ntile = cells // tile
    rows = width // n_dp
    scale = 1.0 / math.sqrt(n_dp * n_rg * cells)
    full = 128
    smem = pl.BlockSpec(memory_space=pltpu.SMEM)
    vmem = pl.BlockSpec(memory_space=pltpu.VMEM)
    hbm = pl.BlockSpec(memory_space=pl.ANY)
    dma = pltpu.SemaphoreType.DMA
    out, gf, sm, su = pl.pallas_call(
        functools.partial(kernel, n_dp, n_rg, scale),
        out_shape=(
            jax.ShapeDtypeStruct((ntile, tile, width), BF16),
            jax.ShapeDtypeStruct((ntile, tile, width), BF16),
            jax.ShapeDtypeStruct((width, width), F32),
            jax.ShapeDtypeStruct((width, width), F32),
        ),
        in_specs=[smem, smem, smem, vmem, vmem, hbm, hbm, hbm, vmem, vmem],
        out_specs=(hbm, hbm, vmem, vmem),
        scratch_shapes=[
            pltpu.VMEM((ntile, tile, width), BF16),
            pltpu.VMEM((slots, tile, tile), BF16),
            pltpu.VMEM((ntile, tile, width), BF16),
            pltpu.VMEM((ntile + 2 * bound, tile, width), BF16),
            pltpu.VMEM((2 * bound, tile, width), BF16),
            pltpu.VMEM((2 * bound, tile, width), BF16),
            pltpu.VMEM((slots + 1, tile, width), F32),
            pltpu.VMEM((ntile, tile, width), BF16),
            pltpu.VMEM((ntile, tile, width), BF16),
            pltpu.VMEM((ntile, tile, width), BF16),
            pltpu.VMEM((2 * bound, tile, width), BF16),
            pltpu.VMEM((2 * bound + 1, tile, width), BF16),
            pltpu.VMEM((8, full), jnp.int32),
            pltpu.VMEM((16, full), jnp.int32),
            pltpu.SMEM((16, full), jnp.int32),
            pltpu.VMEM((2, width, width), F32),
            pltpu.VMEM((2, width, width), WIRE),
            pltpu.VMEM((2, n_dp - 1, rows, width), WIRE),
            pltpu.VMEM((2, n_rg, rows, width), WIRE),
            pltpu.VMEM((2, n_dp, rows, width), WIRE),
            dma((3,)),
            dma,
            dma((2,)),
            dma((2,)),
            dma((2,)),
            dma((2,)),
            dma((2,)),
            dma((2, n_dp - 1)),
            dma((2, n_dp - 1)),
            dma((2, n_rg - 1)),
            dma((2, n_rg - 1)),
            dma((2, n_dp - 1)),
            dma((2, n_dp - 1)),
        ],
        compiler_params=pltpu.CompilerParams(
            collective_id=0, has_side_effects=True, vmem_limit_bytes=56 * 1024 * 1024
        ),
    )(counts, send_low, send_high, src_tiles, dst_tiles, features.reshape(ntile, tile, width),
      adjacency[0], grad_out.reshape(ntile, tile, width),
      w_message, w_update)
    return out.reshape(features.shape), gf.reshape(features.shape), sm, su


def solution(mesh):
    in_specs = (
        P(("groups", "dp"), "region", None),
        P(("groups", "dp"), "region", None, None),
        P(("groups", "dp"), "region"),
        P(("groups", "dp"), "region"),
        P(("groups", "dp"), "region"),
        P(("groups", "dp"), "region"),
        P(("groups", "dp"), "region"),
        P(),
        P(),
        P(("groups", "dp"), "region", None),
    )
    out_specs = (
        P(("groups", "dp"), "region", None),
        P(("groups", "dp"), "region", None),
        P("groups", None),
        P("groups", None),
    )
    n_dp, n_rg = mesh.shape["dp"], mesh.shape["region"]
    return jax.shard_map(
        functools.partial(body, n_dp, n_rg), mesh=mesh, in_specs=in_specs, out_specs=out_specs,
        check_vma=False,
    )
```

time: 308 us -> 69.6 us (0.23)
  waiting for transfers between devices: 106 us -> 0 us
  other arithmetic: 73.9 us -> 0 us
  Pallas kernels: 0 us -> 62.2 us
  local copies, waits for them, and re-layouts: 64.3 us -> 5.93 us
  matrix products: 38.2 us -> 0 us
  between operations: 14.8 us -> 1.3 us
  starting transfers between devices: 8.93 us -> 0 us
    psum x1 -> x0, waiting for transfers between devices: 85.5 us -> none  [body(): lax.psum((part_message, part_update), ('dp', 'region'))]
    scatter-add x4 -> x0, other arithmetic: 62.8 us -> none  [the longest x1 28.8 us: body(): grad_ext = jnp.zeros((ntile + 2 * bound, tile, width), jnp.float32).at[sr...]
    pallas_call x0 -> x1, Pallas kernels: none -> 62.2 us  [body(): pl.pallas_call(functools.partial(kernel, n_dp, n_rg, scale), out_shape=(j...]
    dot_general x8 -> x0, matrix products: 38.2 us -> none  [the longest x1 9.85 us: body(): jnp.einsum('kij,kid->kjd', adj, picked, preferred_element_type=jnp.float32)]
    mul x2 -> x0, local copies, waits for them, and re-layouts: 25.2 us -> none  [the longest x1 12.6 us: body(): contrib * live[:, None, None]]
    gather x4 -> x0, local copies, waits for them, and re-layouts: 21 us -> none  [the longest x1 7.72 us: body(): gathered = extended[src]]
    ppermute x4 -> x0, waiting for transfers between devices: 21 us -> none  [the longest x2 10.6 us: with_halo(): lax.ppermute(head, axis, [((i + 1) % count, i) for i in range(count)])]
    ppermute x4 -> x0, starting transfers between devices: 8.89 us -> none  [the longest x2 5.5 us: with_halo(): lax.ppermute(head, axis, [((i + 1) % count, i) for i in range(count)])]
  transfers between devices with their start and end apart: 5 -> 0, of which waited for: 5 -> 0; matrix products, arithmetic and copies ran while one was open for 5% -> 0% of each run, Pallas kernels for 0% -> 0%
where the time goes in v1:
time: 69.6 us; the launch traced here: 69.5 us
  Pallas kernels  62.2 us (89%)
  local copies, waits for them, and re-layouts  5.93 us (9%)
  between operations  1.3 us (2%)
    pallas_call x1, Pallas kernels, body(): pl.pallas_call(functools.partial(kernel, n_dp, n_rg, scale), out_shape=(j...  62.2 us
    unnamed x10, local copies, waits for them, and re-layouts  5.93 us

profile of v1, /device:TPU:0, one launch (start us, length us, event | category | flops | bytes accessed | tf_op | source)
XLA Modules:
  0.0 69.5 jit_solution(11638145054145637998)
XLA Ops:
  1.3 62.2 %shard_map.129 = (bf16[32,128,256]{2,1,0:T(8,128)(2,1)}, bf16[32,128,256]{2,1,0:T(8,128)(2,1)}, f32[256,256]{1,0:T(8,128)}, f32[256,256]{1,0:T(8,128)}) custom-call(s32[1,1]{1,0:T(1,128)S(6)} %copy.18.counts, s32[1,4]{1,0:T(1,128)} %lows.1, s32[1,4]{1,0:T(1,128)} %highs.1, s32[1,96]{1,0:T(1,128)} %src_ref.1, s32[1,96]{1,0:T(1,128)} %dst_ref.1, ...), custom_call_target="tpu_custom_call" | custom-call | tf_op jit(solution)/shard_map/pallas_call | solution.py:340
  63.5 0.0 copy-start
  63.5 3.2 %copy.19 = bf16[1,4096,256]{2,1,0:T(8,128)(2,1)} copy(bf16[1,4096,256]{2,1,0:T(8,128)(2,1)} %bitcast.9) | data formatting | bytes 4194304
  66.7 0.0 copy-done
  66.7 0.0 copy-start.2
  66.7 0.0 copy-start.1
  66.7 1.3 %copy.20 = bf16[1,4096,256]{2,1,0:T(8,128)(2,1)} copy(bf16[1,4096,256]{2,1,0:T(8,128)(2,1)S(1)} %bitcast.8) | data formatting | bytes 4194304
  68.1 0.0 copy-done.2
  68.1 0.7 %copy.21 = f32[256,256]{1,0:T(8,128)} copy(f32[256,256]{1,0:T(8,128)S(1)} %copy-done.2) | data formatting | bytes 524288
  68.8 0.0 copy-done.1
  68.8 0.7 %copy.22 = f32[256,256]{1,0:T(8,128)} copy(f32[256,256]{1,0:T(8,128)S(1)} %copy-done.1) | data formatting | bytes 524288
Async XLA Ops:
  63.5 3.2 %copy-start = (bf16[32,128,256]{2,1,0:T(8,128)(2,1)S(1)}, bf16[32,128,256]{2,1,0:T(8,128)(2,1)}, u32[]{:S(2)}) copy-start(bf16[32,128,256]{2,1,0:T(8,128)(2,1)} %get-tuple-element.9) | copy-start | bytes 6291460
  66.7 1.3 %copy-start.2 = (f32[256,256]{1,0:T(8,128)S(1)}, f32[256,256]{1,0:T(8,128)}, u32[]{:S(2)}) copy-start(f32[256,256]{1,0:T(8,128)} %get-tuple-element.18) | copy-start | bytes 786436
  66.7 2.0 %copy-start.1 = (f32[256,256]{1,0:T(8,128)S(1)}, f32[256,256]{1,0:T(8,128)}, u32[]{:S(2)}) copy-start(f32[256,256]{1,0:T(8,128)} %get-tuple-element.19) | copy-start | bytes 786436

commit v2 on v1

--- a/solution.py
+++ b/solution.py
@@ -51,8 +51,8 @@
     g_hbm,
     wm,
     wu,
-    out_hbm,
-    gf_hbm,
+    out_v,
+    gf_v,
     sm_ref,
     su_ref,
     x,
@@ -63,8 +63,6 @@
     sent,
     runs,
     gagg,
-    out_v,
-    gf_v,
     rim_s,
     rim_r,
     pad,
@@ -77,7 +75,6 @@
     wire3,
     load_sem,
     tab_sem,
-    store_sem,
     hs_sem,
     hr_sem,
     bs_sem,
@@ -110,17 +107,15 @@
         pl.semaphore_signal(barrier, inc=1, device_id={"dp": lax.rem(dp + off, n_dp)}, device_id_type=MESH)
     for off in range(1, n_rg):
         pl.semaphore_signal(barrier, inc=1, device_id={"region": lax.rem(rg + off, n_rg)}, device_id_type=MESH)
-    pl.semaphore_wait(barrier, n_dp + n_rg - 2)
-
     loads[0].wait()
     for i in range(bound):
         sent[bound + i] = x[highs[0, i]]
+        sent[i] = x[lows[0, i]]
+    pl.semaphore_wait(barrier, n_dp + n_rg - 2)
     to_up = pltpu.make_async_remote_copy(
         sent.at[pl.ds(bound, bound)], halo.at[pl.ds(0, bound)], hs_sem.at[0], hr_sem.at[0],
         device_id={"region": up}, device_id_type=MESH)
     to_up.start()
-    for i in range(bound):
-        sent[i] = x[lows[0, i]]
     to_down = pltpu.make_async_remote_copy(
         sent.at[pl.ds(0, bound)], halo.at[pl.ds(bound, bound)], hs_sem.at[1], hr_sem.at[1],
         device_id={"region": down}, device_id_type=MESH)
@@ -186,19 +181,17 @@
     total[0] = jnp.zeros((width, width), F32)
 
     def middle(c, _):
-        at = pl.ds(2 * c, 2)
-        agg = jnp.concatenate([runs[tab[3, 2 * c]], runs[tab[3, 2 * c + 1]]], axis=0).astype(BF16)
+        at = pl.ds(4 * c, 4)
+        agg = jnp.concatenate([runs[tab[3, 4 * c + u]] for u in range(4)], axis=0).astype(BF16)
         update = dot(agg, wu[...])
-        sig = jax.nn.sigmoid(update)
+        sig = 0.5 * jnp.tanh(0.5 * update) + 0.5
         out_v[at] = tiles_of((rows_of(x[at]).astype(F32) + update * sig).astype(BF16))
         gin = (rows_of(g[at]).astype(F32) * sig * (1.0 + update * (1.0 - sig))).astype(BF16)
         total[0] += dot(agg, gin, 0, 0)
         gagg[at] = tiles_of(dot(gin, wu[...], 1, 1).astype(BF16))
         return 0
 
-    lax.fori_loop(0, ntile // 2, middle, 0)
-    store_out = pltpu.make_async_copy(out_v, out_hbm, store_sem.at[0])
-    store_out.start()
+    lax.fori_loop(0, ntile // 4, middle, 0)
 
     def my_rows(d):
         return pl.ds(pl.multiple_of(d * rows, rows), rows)
@@ -261,7 +254,10 @@
             runs[j + 1] = acc
         return 0
 
-    lax.fori_loop(0, slots // GROUP, backward, 0)
+    half = slots // GROUP // 2
+    lax.fori_loop(0, half, backward, 0)
+    u2 = across(0, u1)
+    lax.fori_loop(half, slots // GROUP, backward, 0)
     for i in range(2 * bound):
         rim_s[i] = runs[tab[7, ntile + i]].astype(BF16)
     rim_down = pltpu.make_async_remote_copy(
@@ -272,28 +268,28 @@
         device_id={"region": up}, device_id_type=MESH)
     rim_down.start()
     rim_up.start()
-    u2 = across(0, u1)
-
-    total[1] = jnp.zeros((width, width), F32)
+    total[1] = dot(rows_of(halo[...]), rows_of(rim_s[...]), 0, 0)
 
     def own(c, _):
-        at = pl.ds(2 * c, 2)
-        gm = jnp.concatenate([runs[tab[7, 2 * c]], runs[tab[7, 2 * c + 1]]], axis=0).astype(BF16)
+        at = pl.ds(4 * c, 4)
+        gm = jnp.concatenate([runs[tab[7, 4 * c + u]] for u in range(4)], axis=0).astype(BF16)
         total[1] += dot(rows_of(x[at]), gm, 0, 0)
         return 0
 
-    lax.fori_loop(0, ntile // 2, own, 0)
+    lax.fori_loop(0, ntile // 4, own, 0)
+    m1 = spread(1)
     u3 = back(0, u2)
+    m2 = across(1, m1)
+    finish(0, u3, su_ref)
+    m3 = back(1, m2)
     rim_down.wait()
     rim_up.wait()
-    total[1] += dot(rows_of(sent[...]), rows_of(rim_r[pl.ds(0, 2 * bound)]), 0, 0)
-    m1 = spread(1)
 
     def features(c):
-        at = pl.ds(2 * c, 2)
+        at = pl.ds(4 * c, 4)
         parts = []
-        for u in range(2):
-            t = 2 * c + u
+        for u in range(4):
+            t = 4 * c + u
             parts.append(
                 runs[tab[7, t]]
                 + rim_r[tab[8, t]].astype(F32)
@@ -302,26 +298,12 @@
         gm = jnp.concatenate(parts, axis=0).astype(BF16)
         gf_v[at] = tiles_of((rows_of(g[at]).astype(F32) + dot(gm, wm[...], 1, 1)).astype(BF16))
 
-    pairs = ntile // 2
-    third = pairs // 3
-
-    def some(lo_, hi_):
-        def step(c, _):
-            features(c)
-            return 0
-
-        lax.fori_loop(lo_, hi_, step, 0)
-
-    some(0, third)
-    m2 = across(1, m1)
-    some(third, pairs)
-    store_gf = pltpu.make_async_copy(gf_v, gf_hbm, store_sem.at[1])
-    store_gf.start()
-    finish(0, u3, su_ref)
-    m3 = back(1, m2)
+    def step(c, _):
+        features(c)
+        return 0
+
+    lax.fori_loop(0, ntile // 4, step, 0)
     finish(1, m3, sm_ref)
-    store_out.wait()
-    store_gf.wait()
 
 
 def body(n_dp, n_rg, features, adjacency, src_tiles, dst_tiles, counts, send_low, send_high,
@@ -340,13 +322,13 @@
     out, gf, sm, su = pl.pallas_call(
         functools.partial(kernel, n_dp, n_rg, scale),
         out_shape=(
-            jax.ShapeDtypeStruct((ntile, tile, width), BF16),
-            jax.ShapeDtypeStruct((ntile, tile, width), BF16),
-            jax.ShapeDtypeStruct((width, width), F32),
-            jax.ShapeDtypeStruct((width, width), F32),
+            pltpu.VMEM((ntile, tile, width), BF16),
+            pltpu.VMEM((ntile, tile, width), BF16),
+            pltpu.VMEM((width, width), F32),
+            pltpu.VMEM((width, width), F32),
         ),
         in_specs=[smem, smem, smem, vmem, vmem, hbm, hbm, hbm, vmem, vmem],
-        out_specs=(hbm, hbm, vmem, vmem),
+        out_specs=(vmem, vmem, vmem, vmem),
         scratch_shapes=[
             pltpu.VMEM((ntile, tile, width), BF16),
             pltpu.VMEM((slots, tile, tile), BF16),
@@ -355,8 +337,6 @@
             pltpu.VMEM((2 * bound, tile, width), BF16),
             pltpu.VMEM((2 * bound, tile, width), BF16),
             pltpu.VMEM((slots + 1, tile, width), F32),
-            pltpu.VMEM((ntile, tile, width), BF16),
-            pltpu.VMEM((ntile, tile, width), BF16),
             pltpu.VMEM((ntile, tile, width), BF16),
             pltpu.VMEM((2 * bound, tile, width), BF16),
             pltpu.VMEM((2 * bound + 1, tile, width), BF16),
@@ -374,7 +354,6 @@
             dma((2,)),
             dma((2,)),
             dma((2,)),
-            dma((2,)),
             dma((2, n_dp - 1)),
             dma((2, n_dp - 1)),
             dma((2, n_rg - 1)),
@@ -383,7 +362,7 @@
             dma((2, n_dp - 1)),
         ],
         compiler_params=pltpu.CompilerParams(
-            collective_id=0, has_side_effects=True, vmem_limit_bytes=56 * 1024 * 1024
+            collective_id=0, has_side_effects=True, vmem_limit_bytes=48 * 1024 * 1024
         ),
     )(counts, send_low, send_high, src_tiles, dst_tiles, features.reshape(ntile, tile, width),
       adjacency[0], grad_out.reshape(ntile, tile, width),

time: 69.6 us -> 62.2 us (0.89)
  Pallas kernels: 62.2 us -> 52.3 us
  local copies, waits for them, and re-layouts: 5.93 us -> 8.46 us
    pallas_call x1, Pallas kernels: 62.2 us -> 52.3 us  [body(): pl.pallas_call(functools.partial(kernel, n_dp, n_rg, scale), out_shape=(p...]
    unnamed x10 -> x16, local copies, waits for them, and re-layouts: 5.93 us -> 8.46 us
where the time goes in v2:
time: 62.2 us; the launch traced here: 62 us
  Pallas kernels  52.3 us (84%)
  local copies, waits for them, and re-layouts  8.46 us (14%)
  between operations  1.3 us (2%)
    pallas_call x1, Pallas kernels, body(): pl.pallas_call(functools.partial(kernel, n_dp, n_rg, scale), out_shape=(p...  52.3 us
    unnamed x16, local copies, waits for them, and re-layouts  8.46 us

profile of v2, /device:TPU:0, one launch (start us, length us, event | category | flops | bytes accessed | tf_op | source)
XLA Modules:
  0.0 62.0 jit_solution(10442207965910593327)
XLA Ops:
  1.3 0.0 copy-start
  1.3 0.9 %copy-done = bf16[256,256]{1,0:T(8,128)(2,1)S(1)} copy-done((bf16[256,256]{1,0:T(8,128)(2,1)S(1)}, bf16[256,256]{1,0:T(8,128)(2,1)}, u32[]{:S(2)}) %copy-start) | copy-done | bytes 131096
  2.2 0.0 copy-start.1
  2.2 0.9 %copy-done.1 = bf16[256,256]{1,0:T(8,128)(2,1)S(1)} copy-done((bf16[256,256]{1,0:T(8,128)(2,1)S(1)}, bf16[256,256]{1,0:T(8,128)(2,1)}, u32[]{:S(2)}) %copy-start.1) | copy-done | bytes 131096
  3.1 0.0 copy-start.2
  3.1 0.7 %copy-done.2 = s32[1,4]{1,0:T(1,128)S(1)} copy-done((s32[1,4]{1,0:T(1,128)S(1)}, s32[1,4]{1,0:T(1,128)}, u32[]{:S(2)}) %copy-start.2) | copy-done | bytes 40
  3.7 0.0 copy-start.3
  3.7 0.7 %copy-done.3 = s32[1,4]{1,0:T(1,128)S(1)} copy-done((s32[1,4]{1,0:T(1,128)S(1)}, s32[1,4]{1,0:T(1,128)}, u32[]{:S(2)}) %copy-start.3) | copy-done | bytes 40
  4.4 0.0 copy-start.4
  4.4 0.7 %copy-done.4 = s32[1,96]{1,0:T(1,128)S(1)} copy-done((s32[1,96]{1,0:T(1,128)S(1)}, s32[1,96]{1,0:T(1,128)}, u32[]{:S(2)}) %copy-start.4) | copy-done | bytes 408
  5.1 0.0 copy-start.5
  5.1 0.7 %copy-done.5 = s32[1,96]{1,0:T(1,128)S(1)} copy-done((s32[1,96]{1,0:T(1,128)S(1)}, s32[1,96]{1,0:T(1,128)}, u32[]{:S(2)}) %copy-start.5) | copy-done | bytes 408
  5.7 52.3 %shard_map.129 = (bf16[32,128,256]{2,1,0:T(8,128)(2,1)S(1)}, bf16[32,128,256]{2,1,0:T(8,128)(2,1)S(1)}, f32[256,256]{1,0:T(8,128)S(1)}, f32[256,256]{1,0:T(8,128)S(1)}) custom-call(s32[1,1]{1,0:T(1,128)S(6)} %copy.22.counts, s32[1,4]{1,0:T(1,128)S(1)} %copy-done.2, s32[1,4]{1,0:T(1,128)S(1)} %copy-done.3, s32[1,96]{1,0:T(1,128)S(1)} %copy-done.4, ...), custom_call_target="tpu_custom_call" | custom-call | tf_op jit(solution)/shard_map/pallas_call | solution.py:322
  58.0 1.3 %copy.18 = bf16[1,4096,256]{2,1,0:T(8,128)(2,1)} copy(bf16[1,4096,256]{2,1,0:T(8,128)(2,1)S(1)} %bitcast.6) | data formatting | bytes 4194304
  59.3 1.3 %copy.19 = bf16[1,4096,256]{2,1,0:T(8,128)(2,1)} copy(bf16[1,4096,256]{2,1,0:T(8,128)(2,1)S(1)} %bitcast.5) | data formatting | bytes 4194304
  60.6 0.7 %copy.20 = f32[256,256]{1,0:T(8,128)} copy(f32[256,256]{1,0:T(8,128)S(1)} %get-tuple-element.14) | data formatting | bytes 524288
  61.3 0.7 %copy.21 = f32[256,256]{1,0:T(8,128)} copy(f32[256,256]{1,0:T(8,128)S(1)} %get-tuple-element.15) | data formatting | bytes 524288
Async XLA Ops:
  1.3 0.9 %copy-start = (bf16[256,256]{1,0:T(8,128)(2,1)S(1)}, bf16[256,256]{1,0:T(8,128)(2,1)}, u32[]{:S(2)}) copy-start(bf16[256,256]{1,0:T(8,128)(2,1)} %wm.1) | copy-start | bytes 393220
  2.2 0.9 %copy-start.1 = (bf16[256,256]{1,0:T(8,128)(2,1)S(1)}, bf16[256,256]{1,0:T(8,128)(2,1)}, u32[]{:S(2)}) copy-start(bf16[256,256]{1,0:T(8,128)(2,1)} %wu.1) | copy-start | bytes 393220
  3.1 0.7 %copy-start.2 = (s32[1,4]{1,0:T(1,128)S(1)}, s32[1,4]{1,0:T(1,128)}, u32[]{:S(2)}) copy-start(s32[1,4]{1,0:T(1,128)} %lows.1) | copy-start | bytes 52
  3.7 0.7 %copy-start.3 = (s32[1,4]{1,0:T(1,128)S(1)}, s32[1,4]{1,0:T(1,128)}, u32[]{:S(2)}) copy-start(s32[1,4]{1,0:T(1,128)} %highs.1) | copy-start | bytes 52
  4.4 0.7 %copy-start.4 = (s32[1,96]{1,0:T(1,128)S(1)}, s32[1,96]{1,0:T(1,128)}, u32[]{:S(2)}) copy-start(s32[1,96]{1,0:T(1,128)} %src_ref.1) | copy-start | bytes 1156
  5.1 0.7 %copy-start.5 = (s32[1,96]{1,0:T(1,128)S(1)}, s32[1,96]{1,0:T(1,128)}, u32[]{:S(2)}) copy-start(s32[1,96]{1,0:T(1,128)} %dst_ref.1) | copy-start | bytes 1156
